TPU v7x, 256 devices: a whole 4x4x8 slice. The times are simulated.
256 devices in a mesh: dp: 16 (over z, y_hi), own: 16 (over y_lo, x, core).
Axes of the slice: x: 4, y: 4 (y_hi: 2, y_lo: 2; y = y_hi * 2 + y_lo), z: 8, core: 2. Of those that a mesh axis runs over, the one named last changes fastest.
Arguments:
- grad_parts: bfloat16 [16, 16, 1152, 1152], P('own', None, 'dp'), may hold values from -4.5 to 4.5
- owner_list: int32 [16], replicated, may hold values from 0 to 15, as said below
- left_stat: float32 [16, 3, 1152, 1152], P('own', None, 'dp'), may hold values from -3 to 3
- right_stat: float32 [16, 3, 1152, 1152], P('own', None, 'dp'), may hold values from -3 to 3
- second_moment: float32 [16, 3, 1152, 1152], P('own', None, 'dp'), may hold values from 0.1 to 10
- left_root: bfloat16 [16, 3, 1152, 1152], P('own', None, 'dp'), may hold values from -3 to 3
- right_root: bfloat16 [16, 3, 1152, 1152], P('own', None, 'dp'), may hold values from -3 to 3
- weights: bfloat16 [16, 3, 1152, 1152], P('own', None, 'dp'), may hold values from -6 to 6
Outputs:
- new_left: float32 [16, 3, 1152, 1152], P('own', None, 'dp')
- new_right: float32 [16, 3, 1152, 1152], P('own', None, 'dp')
- new_second: float32 [16, 3, 1152, 1152], P('own', None, 'dp')
- new_weights: bfloat16 [16, 1152, 1152], P(None, 'dp')
Inputs may be any that keep to these rules, and one draw needn't show every extreme that they name: `owner_list`: no owner index is named by more than 3 blocks, and one is named by exactly 3.
All inputs are finite; a program needn't handle non-finite values.
Results may differ from a plain program's by a relative error of at most 0.02.
Values may be sent and summed in bfloat16 or wider, within the bound.
A program may use at most 128 MiB of HBM per device.

v0:
```python
import jax
import jax.numpy as jnp
from jax import lax
from jax.sharding import PartitionSpec as P


def slot_tables(owner_list, owner_count, slot_count, unit_count):
    index = jnp.arange(unit_count, dtype=jnp.int32)
    earlier = (owner_list[:, None] == owner_list[None, :]) & (index[None, :] < index[:, None])
    rank = jnp.sum(earlier.astype(jnp.int32), axis=1)
    slot_id = owner_list * slot_count + rank
    every_slot = jnp.arange(owner_count * slot_count, dtype=jnp.int32)
    match = (slot_id[None, :] == every_slot[:, None]).astype(jnp.int32)
    unit_of_slot = jnp.sum(match * index[None, :], axis=1)
    filled = jnp.sum(match, axis=1) > 0
    return (slot_id, unit_of_slot, filled)


def local(
    grad_parts, owner_list, left_stat, right_stat, second_moment, left_root, right_root, weights
):
    owner_count = lax.axis_size("own")
    row_index = lax.axis_index("dp")
    slot_count = left_stat.shape[1]
    block_rows = left_stat.shape[2]
    width = left_stat.shape[3]
    unit_count = owner_list.shape[0]
    slot_id, unit_of_slot, filled = slot_tables(owner_list, owner_count, slot_count, unit_count)
    parts = grad_parts[0]
    packed = jnp.take(parts, unit_of_slot, axis=0)
    packed = jnp.where(filled[:, None, None], packed.astype(jnp.float32), jnp.float32(0.0))
    summed = lax.psum_scatter(packed.astype(jnp.bfloat16), "own", scatter_dimension=0, tiled=True)
    my_columns = row_index * block_rows
    lefts, rights, seconds, preconds, adam_sums, pre_sums = ([], [], [], [], [], [])
    for slot_pos in range(slot_count):
        grad_rows = summed[slot_pos]
        root_rows = left_root[0, slot_pos]
        piece = lax.all_gather(grad_rows, "dp", axis=0, tiled=True)
        block = lax.dot_general(
            grad_rows, piece, (((1,), (1,)), ((), ())), preferred_element_type=jnp.float32
        )
        own_cols = lax.dynamic_slice_in_dim(piece, my_columns, block_rows, 1)
        right_rows = lax.dot_general(
            own_cols, piece, (((0,), (0,)), ((), ())), preferred_element_type=jnp.float32
        )
        mixed_rows = jnp.dot(root_rows, piece, preferred_element_type=jnp.float32)
        mixed_half = mixed_rows.astype(jnp.bfloat16)
        precond = jnp.dot(
            mixed_half,
            lax.all_gather(right_root[0, slot_pos], "dp", axis=0, tiled=True),
            preferred_element_type=jnp.float32,
        )
        lefts.append(0.95 * left_stat[0, slot_pos] + 0.05 / width * block)
        rights.append(0.95 * right_stat[0, slot_pos] + 0.05 / width * right_rows)
        gradient = grad_rows.astype(jnp.float32)
        second_new = 0.95 * second_moment[0, slot_pos] + 0.05 * gradient * gradient
        seconds.append(second_new)
        adam = gradient / (jnp.sqrt(second_new) + 1e-08)
        adam_sums.append(jnp.sum(adam * adam))
        pre_sums.append(jnp.sum(precond * precond))
        preconds.append(precond)
    adam_total, pre_total = lax.psum((jnp.stack(adam_sums), jnp.stack(pre_sums)), "dp")
    graft = jnp.sqrt(adam_total / (pre_total + 1e-06))
    stacked = jnp.stack(preconds)
    new_rows = (weights[0].astype(jnp.float32) - 0.3 * graft[:, None, None] * stacked).astype(
        jnp.bfloat16
    )
    every_rows = lax.all_gather(new_rows, "own", axis=0, tiled=True)
    new_weights = jnp.take(every_rows, slot_id, axis=0)
    new_left = jnp.stack(lefts)[None]
    new_right = jnp.stack(rights)[None]
    new_second = jnp.stack(seconds)[None]
    return (new_left, new_right, new_second, new_weights)


def solution(mesh):
    in_specs = (
        P("own", None, "dp", None),
        P(),
        P("own", None, "dp", None),
        P("own", None, "dp", None),
        P("own", None, "dp", None),
        P("own", None, "dp", None),
        P("own", None, "dp", None),
        P("own", None, "dp", None),
    )
    out_specs = (
        P("own", None, "dp", None),
        P("own", None, "dp", None),
        P("own", None, "dp", None),
        P(None, "dp", None),
    )
    return jax.shard_map(local, mesh=mesh, in_specs=in_specs, out_specs=out_specs, check_vma=False)
```

profile of v0, /device:TPU:1, one launch (start us, length us, event | category | flops | bytes accessed | tf_op | source)
XLA Modules:
  0.0 739.3 jit_solution(6900974425254003692)
XLA Ops:
  9.9 5.7 gather_fusion
  15.6 11.3 %select_convert_fusion = bf16[48,72,1152]{2,1,0:T(8,128)(2,1)} fusion(bf16[48,72,1152]{2,1,0:T(8,128)(2,1)} %gather_fusion, pred[48]{0:T(512)(128)(4,1)S(1)} %get-tuple-element.28, pred[48]{0:T(512)(128)(4,1)S(1)} %get-tuple-element.29), kind=kLoop, calls=%fused_computation.2 | loop fusion | flops 15925248 | bytes 15925344 | tf_op jit(solution)/shard_map/convert_element_type | solution.py:32
  30.0 146.8 %all-reduce.4.cloned.1.call-done = bf16[48,72,1152]{2,1,0:T(8,128)(2,1)} async-done(((bf16[48,72,1152]{2,1,0:T(8,128)(2,1)}), bf16[48,72,1152]{2,1,0:T(8,128)(2,1)}) %all-reduce.4.cloned.1.call-update) | async-done | bytes 7962640
  176.8 3.0 fusion.112
  182.7 2.0 pad_maximum_fusion
  184.7 82.4 %all-gather.20.cloned.1.call-done = bf16[1,1152,1152]{2,1,0:T(8,128)(2,1)} async-done(((bf16[1,72,1152]{2,1,0:T(8,128)(2,1)}), bf16[1,1152,1152]{2,1,0:T(8,128)(2,1)}) %all-gather.20.cloned.1.call-update) | async-done | bytes 2654224 | tf_op jit(solution)/shard_map/all_gather | solution.py:38
  267.1 4.2 multiply_reduce_fusion
  271.3 84.0 %all-gather.24.cloned.1.call-done = bf16[1,1,1152,1152]{3,2,1,0:T(8,128)(2,1)} async-done(((bf16[1,1,72,1152]{3,2,1,0:T(8,128)(2,1)}), bf16[1,1,1152,1152]{3,2,1,0:T(8,128)(2,1)}) %all-gather.24.cloned.1.call-update) | async-done | bytes 2654224 | tf_op jit(solution)/shard_map/all_gather | solution.py:50
  355.3 89.0 %all-gather.18.cloned.1.call-done = bf16[1,1152,1152]{2,1,0:T(8,128)(2,1)} async-done(((bf16[1,72,1152]{2,1,0:T(8,128)(2,1)}), bf16[1,1152,1152]{2,1,0:T(8,128)(2,1)}) %all-gather.18.cloned.1.call-update) | async-done | bytes 2654224 | tf_op jit(solution)/shard_map/all_gather | solution.py:38
  444.3 4.3 multiply_reduce_fusion.1
  448.6 84.7 %all-gather.22.cloned.1.call-done = bf16[1,1,1152,1152]{3,2,1,0:T(8,128)(2,1)} async-done(((bf16[1,1,72,1152]{3,2,1,0:T(8,128)(2,1)}), bf16[1,1,1152,1152]{3,2,1,0:T(8,128)(2,1)}) %all-gather.22.cloned.1.call-update) | async-done | bytes 2654224 | tf_op jit(solution)/shard_map/all_gather | solution.py:50
  533.3 89.0 %all-gather.16.cloned.1.call-done = bf16[1,1152,1152]{2,1,0:T(8,128)(2,1)} async-done(((bf16[1,72,1152]{2,1,0:T(8,128)(2,1)}), bf16[1,1152,1152]{2,1,0:T(8,128)(2,1)}) %all-gather.16.cloned.1.call-update) | async-done | bytes 2654224 | tf_op jit(solution)/shard_map/all_gather | solution.py:38
  622.2 4.2 multiply_reduce_fusion.2
  626.5 2.0 pad_maximum_fusion.1
  628.4 31.3 %all-reduce.1 = (f32[3]{0:T(128)S(1)}, f32[3]{0:T(128)S(1)}) all-reduce(f32[3]{0:T(128)S(1)} %pad_maximum_fusion, f32[3]{0:T(128)S(1)} %pad_maximum_fusion.1), channel_id=1, replica_groups=mesh['dp'=16,'own'=16] {'dp'}, use_global_device_ids=true, to_apply=%region_7.8 | all-reduce | flops 6 | bytes 48 | tf_op jit(solution)/shard_map/psum | solution.py:62
  660.8 1.5 fusion.98
  662.3 1.0 maximum_bitcast_fusion.2
  666.2 1.0 fusion.66
  667.2 1.0 fusion.63
  668.2 1.0 fusion.60
  669.3 1.0 maximum_bitcast_fusion
  671.3 51.2 %all-gather.14.cloned.1.call-done = bf16[48,72,1152]{2,1,0:T(8,128)(2,1)} async-done(((bf16[3,72,1152]{2,1,0:T(8,128)(2,1)}), bf16[48,72,1152]{2,1,0:T(8,128)(2,1)}) %all-gather.14.cloned.1.call-update) | async-done | bytes 7962640 | tf_op jit(solution)/shard_map/all_gather | solution.py:68
  722.5 5.6 gather_fusion.1
  728.1 3.7 broadcast_select_fusion
  (63 shorter events, 11.9 us)
Async XLA Ops:
  8.0 1.9 copy-start
  8.0 168.8 %all-reduce.4.cloned.1.call-start = ((), (), s32[]{:S(2)}) async-start(), calls=%async_computation.7 | async-start | bytes 15925248
  26.9 1.0 copy-start.12
  26.9 1.9 copy-start.14
  26.9 149.9 %copy-start.5 = (f32[1,3,72,1152]{3,2,1,0:T(8,128)S(1)}, f32[1,3,72,1152]{3,2,1,0:T(8,128)}, u32[]{:S(2)}) copy-start(f32[1,3,72,1152]{3,2,1,0:T(8,128)} %param.12) | copy-start | bytes 2985988
  26.9 240.2 %copy-start.11 = (bf16[1,3,72,1152]{3,2,1,0:T(8,128)(2,1)S(1)}, bf16[1,3,72,1152]{3,2,1,0:T(8,128)(2,1)}, u32[]{:S(2)}) copy-start(bf16[1,3,72,1152]{3,2,1,0:T(8,128)(2,1)} %param.13) | copy-start | bytes 1492996
  26.9 157.8 %all-gather.26.cloned.1.call-start = ((), (), s32[]{:S(2)}) async-start(), calls=%async_computation.6 | async-start | bytes 2820096 | tf_op jit(solution)/shard_map/all_gather | solution.py:50
  28.7 238.3 %all-gather.20.cloned.1.call-start = ((), (), s32[]{:S(2)}) async-start(), calls=%async_computation.3 | async-start | bytes 2820096 | tf_op jit(solution)/shard_map/all_gather | solution.py:38
  179.8 175.5 %all-gather.24.cloned.1.call-start = ((), (), s32[]{:S(2)}) async-start(), calls=%async_computation.5 | async-start | bytes 2820096 | tf_op jit(solution)/shard_map/all_gather | solution.py:50
  180.4 263.9 %all-gather.18.cloned.1.call-start = ((), (), s32[]{:S(2)}) async-start(), calls=%async_computation.2 | async-start | bytes 2820096 | tf_op jit(solution)/shard_map/all_gather | solution.py:38
  181.1 352.1 %all-gather.22.cloned.1.call-start = ((), (), s32[]{:S(2)}) async-start(), calls=%async_computation.4 | async-start | bytes 2820096 | tf_op jit(solution)/shard_map/all_gather | solution.py:50
  181.9 440.4 %all-gather.16.cloned.1.call-start = ((), (), s32[]{:S(2)}) async-start(), calls=%async_computation.1 | async-start | bytes 2820096 | tf_op jit(solution)/shard_map/all_gather | solution.py:38
  182.6 539.9 %all-gather.14.cloned.1.call-start = ((), (), s32[]{:S(2)}) async-start(), calls=%async_computation | async-start | bytes 8460288 | tf_op jit(solution)/shard_map/all_gather | solution.py:68
  448.6 211.1 %copy-start.13 = (bf16[1,3,72,1152]{3,2,1,0:T(8,128)(2,1)S(1)}, bf16[1,3,72,1152]{3,2,1,0:T(8,128)(2,1)}, u32[]{:S(2)}) copy-start(bf16[1,3,72,1152]{3,2,1,0:T(8,128)(2,1)} %param.15) | copy-start | bytes 1492996
  626.4 34.3 %copy-start.6 = (bf16[1,72,1152]{2,1,0:T(8,128)(2,1)S(1)}, bf16[1,72,1152]{2,1,0:T(8,128)(2,1)}, u32[]{:S(2)}) copy-start(bf16[1,72,1152]{2,1,0:T(8,128)(2,1)} %get-tuple-element.13) | copy-start | bytes 497668
  626.4 34.3 %copy-start.7 = (bf16[1,72,1152]{2,1,0:T(8,128)(2,1)S(1)}, bf16[1,72,1152]{2,1,0:T(8,128)(2,1)}, u32[]{:S(2)}) copy-start(bf16[1,72,1152]{2,1,0:T(8,128)(2,1)} %get-tuple-element.14) | copy-start | bytes 497668
  626.4 34.3 %copy-start.8 = (bf16[1,72,1152]{2,1,0:T(8,128)(2,1)S(1)}, bf16[1,72,1152]{2,1,0:T(8,128)(2,1)}, u32[]{:S(2)}) copy-start(bf16[1,72,1152]{2,1,0:T(8,128)(2,1)} %get-tuple-element.15) | copy-start | bytes 497668
  660.7 2.7 copy-start.2
  660.7 2.6 copy-start.10
  662.3 2.3 copy-start.3
  663.4 2.0 copy-start.4
  664.6 1.5 copy-start.9
  728.1 3.7 copy-start.1
Sparse Core Ops, SparseCore 0:
  27.0 149.7 all-reduce.3
  660.9 61.5 all-gather.13
Sparse Core Ops, SparseCore 1:
  30.0 104.8 all-gather.25
  179.9 87.1 all-gather.19
  269.5 85.7 all-gather.23
  358.5 85.7 all-gather.17
  447.5 85.7 all-gather.21
  536.5 85.7 all-gather.15
where the time goes:
time: 740 us; the launch traced here: 739 us
  waiting for transfers between devices  630 us (85%)
  blocking collectives  31.3 us (4%)
  other arithmetic  29.3 us (4%)
  matrix products  18.1 us (2%)
  between operations  16.4 us (2%)
  local copies, waits for them, and re-layouts  14.2 us (2%)
    all_gather x3, waiting for transfers between devices, local(): piece = lax.all_gather(grad_rows, 'dp', axis=0, tiled=True)  260 us
    all_gather x3, waiting for transfers between devices, local(): lax.all_gather(right_root[0, slot_pos], 'dp', axis=0, tiled=True)  169 us
    unnamed x9, waiting for transfers between devices  149 us
    all_gather x1, waiting for transfers between devices, local(): every_rows = lax.all_gather(new_rows, 'own', axis=0, tiled=True)  51.2 us
    psum x1, blocking collectives, local(): lax.psum((jnp.stack(adam_sums), jnp.stack(pre_sums)), 'dp')  31.3 us
  transfers between devices with their start and end apart: 8, of which 7 were waited for; matrix products, arithmetic and copies ran while one was open for 3% of the time, Pallas kernels for 0%

commit v1 on v0

v1 whole, which is shorter than its diff:
```python
import functools

import jax
import jax.numpy as jnp
from jax import lax
from jax.experimental import pallas as pl
from jax.experimental.pallas import tpu as pltpu
from jax.sharding import PartitionSpec as P

MESH = pl.DeviceIdType.MESH
ROWS = 72
WIDTH = 1152
SLOTS = 3
ZS = 8


class Place:
    def __init__(self):
        self.dp = lax.axis_index("dp")
        self.own = lax.axis_index("own")
        self.z = self.dp // 2
        self.h = self.dp % 2
        self.c = self.own % 2
        self.right = self.at((self.dp + 2) % 16, self.own)
        self.left = self.at((self.dp + 14) % 16, self.own)
        self.pair = self.at(self.dp, self.own + 1 - 2 * self.c)
        self.fourth = self.at((self.dp + 16 + 2 * (1 - 2 * self.c)) % 16, self.own)
        self.swap = self.at(2 * self.z + self.c, self.own - self.c + self.h)
        self.swaps = self.c != self.h

    def at(self, dp, own):
        return {"dp": dp, "own": own}

    def block(self, step, core):
        return 2 * ((self.z + step + ZS) % ZS) + core


def rows(block):
    return pl.ds(pl.multiple_of(block * ROWS, 8), ROWS)


def remote(src, dst, send, recv, device):
    return pltpu.make_async_remote_copy(
        src_ref=src, dst_ref=dst, send_sem=send, recv_sem=recv, device_id=device, device_id_type=MESH
    )


def greet(place, devices):
    barrier = pltpu.get_barrier_semaphore()
    for device in devices:
        pl.semaphore_signal(barrier, inc=1, device_id=device, device_id_type=MESH)

    @pl.when(place.swaps)
    def _():
        pl.semaphore_signal(barrier, inc=1, device_id=place.swap, device_id_type=MESH)

    pl.semaphore_wait(barrier, len(devices) + place.swaps.astype(jnp.int32))


def exchange(place, moves, send, recv):
    @pl.when(place.swaps)
    def _():
        for i, (src, dst) in enumerate(moves):
            remote(src, dst, send.at[i], recv.at[i], place.swap).start()

    @pl.when(jnp.logical_not(place.swaps))
    def _():
        for i, (src, dst) in enumerate(moves):
            pltpu.make_async_copy(src, dst, recv.at[i]).start()


def exchange_wait(place, i, src, dst, send, recv):
    @pl.when(place.swaps)
    def _():
        remote(src, dst, send.at[i], recv.at[i], place.swap).wait()

    @pl.when(jnp.logical_not(place.swaps))
    def _():
        pltpu.make_async_copy(src, dst, recv.at[i]).wait()


class Ring:
    def __init__(self, place, full, sems):
        self.place, self.full = place, full
        self.ring_send, self.ring_recv, self.pair_send, self.pair_recv = sems
        self.started = []

    def send(self, slot, block, send, recv, device):
        window = self.full.at[slot, rows(block)]
        copy = remote(window, window, send, recv, device)
        copy.start()
        self.started.append(copy)

    def arrive(self, slot, block, send, recv):
        window = self.full.at[slot, rows(block)]
        remote(window, window, send, recv, self.place.pair).wait_recv()

    def ring(self, way, hop, slot, block, device):
        self.send(slot, block, self.ring_send.at[way, hop, slot], self.ring_recv.at[way, hop, slot], device)

    def hand(self, index, slot, block):
        self.send(slot, block, self.pair_send.at[index, slot], self.pair_recv.at[index, slot], self.place.pair)

    def begin(self, slot):
        p = self.place
        own = p.block(0, p.c)
        self.ring(0, 0, slot, own, p.right)
        self.ring(1, 0, slot, own, p.left)
        self.hand(0, slot, own)

    def hop(self, k, slot):
        p = self.place
        if k < 4:
            from_left, from_right = p.block(-k, p.c), p.block(k, p.c)
            self.arrive(slot, from_left, self.ring_send.at[0, k - 1, slot], self.ring_recv.at[0, k - 1, slot])
            if k < 3:
                self.ring(0, k, slot, from_left, p.right)
            self.hand(k, slot, from_left)
            self.arrive(slot, from_right, self.ring_send.at[1, k - 1, slot], self.ring_recv.at[1, k - 1, slot])
            if k < 3:
                self.ring(1, k, slot, from_right, p.left)
            else:
                last = p.block(-3 * (1 - 2 * p.c), p.c)
                self.ring(0, 3, slot, last, p.fourth)
            self.hand(3 + k, slot, from_right)
        else:
            far = p.block(4, p.c)
            self.arrive(slot, far, self.ring_send.at[0, 3, slot], self.ring_recv.at[0, 3, slot])
            self.hand(7, slot, far)

    def handed(self, slot):
        p = self.place
        steps = [0, -1, -2, -3, 1, 2, 3, 4]
        for index, step in enumerate(steps):
            self.arrive(slot, p.block(step, 1 - p.c), self.pair_send.at[index, slot], self.pair_recv.at[index, slot])

    def finish(self):
        for copy in self.started:
            copy.wait_send()


RING_SEMS = [
    pltpu.SemaphoreType.DMA((2, 4, SLOTS)),
    pltpu.SemaphoreType.DMA((2, 4, SLOTS)),
    pltpu.SemaphoreType.DMA((8, SLOTS)),
    pltpu.SemaphoreType.DMA((8, SLOTS)),
]


def roots_kernel(left_ref, right_ref, left_out, full_out, swap_send, swap_recv, *sems):
    place = Place()
    greet(place, [place.right, place.left, place.pair])
    moves = [(right_ref.at[s], full_out.at[s, rows(place.dp)]) for s in range(SLOTS)]
    moves += [(left_ref.at[s], left_out.at[s]) for s in range(SLOTS)]
    exchange(place, moves, swap_send, swap_recv)
    ring = Ring(place, full_out, sems)
    for slot in range(SLOTS):
        src, _ = moves[slot]
        exchange_wait(place, slot, src, full_out.at[slot, rows(place.block(0, place.c))], swap_send, swap_recv)
        ring.begin(slot)
    for k in range(1, 5):
        for slot in range(SLOTS):
            ring.hop(k, slot)
    for slot in range(SLOTS):
        ring.handed(slot)
        src, dst = moves[SLOTS + slot]
        exchange_wait(place, SLOTS + slot, src, dst, swap_send, swap_recv)
    ring.finish()


def gather_roots(left_root, right_root):
    anywhere = pl.BlockSpec(memory_space=pl.ANY)
    return pl.pallas_call(
        roots_kernel,
        out_shape=(
            jax.ShapeDtypeStruct((SLOTS, ROWS, WIDTH), jnp.bfloat16),
            jax.ShapeDtypeStruct((SLOTS, WIDTH, WIDTH), jnp.bfloat16),
        ),
        in_specs=[anywhere, anywhere],
        out_specs=(anywhere, anywhere),
        scratch_shapes=[
            pltpu.SemaphoreType.DMA((2 * SLOTS,)),
            pltpu.SemaphoreType.DMA((2 * SLOTS,)),
            *RING_SEMS,
        ],
        compiler_params=pltpu.CompilerParams(collective_id=0, has_side_effects=True),
        cost_estimate=pl.CostEstimate(flops=0, bytes_accessed=100_000_000, transcendentals=0),
        name="gather_roots",
    )(left_root, right_root)


NT = (((1,), (1,)), ((), ()))


def main_kernel(
    grad_ref, left_ref, right_ref, weight_ref, adam_ref,
    gram_left_ref, gram_right_ref, new_ref, full_hbm,
    full, right_full, results, returned, sums, totals,
    swap_send, swap_recv, back_send, back_recv, local_sem, sum_send, sum_recv, *sems
):
    place = Place()
    peers = [place.at((place.dp + d) % 16, place.own) for d in range(1, 16)]
    greet(place, [place.pair, *peers])
    load_right = pltpu.make_async_copy(right_ref, right_full, local_sem.at[0])
    load_right.start()
    moves = [(grad_ref.at[s], full_hbm.at[s, rows(place.dp)]) for s in range(SLOTS)]
    exchange(place, moves, swap_send, swap_recv)
    ring = Ring(place, full_hbm, sems)
    work = place.block(0, place.c)
    for slot in range(SLOTS):
        src, _ = moves[slot]
        exchange_wait(place, slot, src, full_hbm.at[slot, rows(work)], swap_send, swap_recv)
        ring.begin(slot)
    for k in range(1, 5):
        for slot in range(SLOTS):
            ring.hop(k, slot)
    for slot in range(SLOTS):
        ring.handed(slot)
        pltpu.make_async_copy(full_hbm.at[slot], full.at[slot], local_sem.at[1 + slot]).start()
    ring.finish()
    load_right.wait()
    lane = lax.broadcasted_iota(jnp.int32, (ROWS, WIDTH), 1)
    row = lax.broadcasted_iota(jnp.int32, (ROWS, WIDTH), 0)
    pick = jnp.where(lane == row + work * ROWS, 1.0, 0.0).astype(jnp.bfloat16)
    for slot in range(SLOTS):
        pltpu.make_async_copy(full_hbm.at[slot], full.at[slot], local_sem.at[1 + slot]).wait()

    def compute(slot, carry):
        grad = full[slot]
        mine = jnp.dot(pick, grad, preferred_element_type=jnp.float32).astype(jnp.bfloat16)
        results[slot, 0] = lax.dot_general(mine, grad, NT, preferred_element_type=jnp.float32).astype(jnp.bfloat16)
        columns = lax.dot_general(pick, grad, NT, preferred_element_type=jnp.float32).astype(jnp.bfloat16)
        results[slot, 1] = jnp.dot(columns, grad, preferred_element_type=jnp.float32).astype(jnp.bfloat16)
        mixed = jnp.dot(left_ref[slot], grad, preferred_element_type=jnp.float32).astype(jnp.bfloat16)
        precond = jnp.dot(mixed, right_full[slot], preferred_element_type=jnp.float32)
        results[slot, 2] = precond.astype(jnp.bfloat16)
        return carry

    lax.fori_loop(0, SLOTS, compute, 0)
    back = [(results.at[s, i], returned.at[s, i]) for s in range(SLOTS) for i in (2, 0, 1)]
    exchange(place, back, back_send, back_recv)
    for i, (src, dst) in enumerate(back):
        exchange_wait(place, i, src, dst, back_send, back_recv)

    spread = jnp.zeros((8, 128), jnp.float32)
    index = lax.broadcasted_iota(jnp.int32, (8, 128), 0)
    for slot in range(SLOTS):
        precond = returned[slot, 2].astype(jnp.float32)
        spread = spread + jnp.where(index == slot, jnp.sum(precond * precond), 0.0)
    sums[...] = spread + adam_ref[...]
    copies = []
    for d, peer in enumerate(peers):
        copies.append(remote(sums, totals.at[d], sum_send.at[d], sum_recv.at[d], peer))
        copies[-1].start()
    gram_left_ref[...] = returned[:, 0]
    gram_right_ref[...] = returned[:, 1]
    total = sums[...]
    for d, copy in enumerate(copies):
        copy.wait()
        total = total + totals[d]
    for slot in range(SLOTS):
        pre_total, adam_total = total[slot : slot + 1, 0:1], total[slot + 3 : slot + 4, 0:1]
        graft = jnp.sqrt(adam_total / (pre_total + 1e-06))
        precond = returned[slot, 2].astype(jnp.float32)
        new_ref[slot] = (weight_ref[slot].astype(jnp.float32) - 0.3 * graft * precond).astype(jnp.bfloat16)


def precondition(grads, left_rows, right_full, weights, adam):
    anywhere = pl.BlockSpec(memory_space=pl.ANY)
    vmem = pl.BlockSpec(memory_space=pltpu.VMEM)
    small = jax.ShapeDtypeStruct((SLOTS, ROWS, WIDTH), jnp.bfloat16)
    return pl.pallas_call(
        main_kernel,
        out_shape=(small, small, small, jax.ShapeDtypeStruct((SLOTS, WIDTH, WIDTH), jnp.bfloat16)),
        in_specs=[anywhere, vmem, anywhere, vmem, vmem],
        out_specs=(vmem, vmem, vmem, anywhere),
        scratch_shapes=[
            pltpu.VMEM((SLOTS, WIDTH, WIDTH), jnp.bfloat16),
            pltpu.VMEM((SLOTS, WIDTH, WIDTH), jnp.bfloat16),
            pltpu.VMEM((SLOTS, 3, ROWS, WIDTH), jnp.bfloat16),
            pltpu.VMEM((SLOTS, 3, ROWS, WIDTH), jnp.bfloat16),
            pltpu.VMEM((8, 128), jnp.float32),
            pltpu.VMEM((15, 8, 128), jnp.float32),
            pltpu.SemaphoreType.DMA((SLOTS,)),
            pltpu.SemaphoreType.DMA((SLOTS,)),
            pltpu.SemaphoreType.DMA((3 * SLOTS,)),
            pltpu.SemaphoreType.DMA((3 * SLOTS,)),
            pltpu.SemaphoreType.DMA((1 + SLOTS,)),
            pltpu.SemaphoreType.DMA((15,)),
            pltpu.SemaphoreType.DMA((15,)),
            *RING_SEMS,
        ],
        compiler_params=pltpu.CompilerParams(
            collective_id=1, has_side_effects=True, vmem_limit_bytes=60 * 1024 * 1024
        ),
        name="precondition",
    )(grads, left_rows, right_full, weights, adam)


def slot_tables(owner_list, owner_count, slot_count, unit_count):
    index = jnp.arange(unit_count, dtype=jnp.int32)
    earlier = (owner_list[:, None] == owner_list[None, :]) & (index[None, :] < index[:, None])
    rank = jnp.sum(earlier.astype(jnp.int32), axis=1)
    slot_id = owner_list * slot_count + rank
    every_slot = jnp.arange(owner_count * slot_count, dtype=jnp.int32)
    match = (slot_id[None, :] == every_slot[:, None]).astype(jnp.int32)
    unit_of_slot = jnp.sum(match * index[None, :], axis=1)
    filled = jnp.sum(match, axis=1) > 0
    return (slot_id, unit_of_slot, filled)


def local(
    grad_parts, owner_list, left_stat, right_stat, second_moment, left_root, right_root, weights
):
    owner_count = lax.axis_size("own")
    unit_count = owner_list.shape[0]
    slot_id, unit_of_slot, filled = slot_tables(owner_list, owner_count, SLOTS, unit_count)
    me = lax.axis_index("own")
    units = lax.dynamic_slice_in_dim(unit_of_slot, me * SLOTS, SLOTS)
    mine = lax.dynamic_slice_in_dim(filled, me * SLOTS, SLOTS)

    left_rows, right_full = gather_roots(left_root[0], right_root[0])
    summed = lax.psum(grad_parts[0], "own")
    grads = jnp.where(mine[:, None, None], jnp.take(summed, units, axis=0), jnp.bfloat16(0.0))

    gradient = grads.astype(jnp.float32)
    new_second = 0.95 * second_moment[0] + 0.05 * gradient * gradient
    adam = gradient / (jnp.sqrt(new_second) + 1e-08)
    adam_sums = jnp.sum(adam * adam, axis=(1, 2))
    adam_tile = jnp.broadcast_to(jnp.pad(adam_sums, (3, 2))[:, None], (8, 128))

    gram_left, gram_right, new_rows, _ = precondition(grads, left_rows, right_full, weights[0], adam_tile)
    scale = 0.05 / WIDTH
    new_left = 0.95 * left_stat + scale * gram_left.astype(jnp.float32)[None]
    new_right = 0.95 * right_stat + scale * gram_right.astype(jnp.float32)[None]
    every_rows = lax.all_gather(new_rows, "own", axis=0, tiled=True)
    new_weights = jnp.take(every_rows, slot_id, axis=0)
    return (new_left, new_right, new_second[None], new_weights)


def solution(mesh):
    placed = P("own", None, "dp", None)
    in_specs = (placed, P(), placed, placed, placed, placed, placed, placed)
    out_specs = (placed, placed, placed, P(None, "dp", None))
    return jax.shard_map(local, mesh=mesh, in_specs=in_specs, out_specs=out_specs, check_vma=False)
```

time: 740 us -> 309 us (0.42)
  waiting for transfers between devices: 630 us -> 127 us
  Pallas kernels: 0 us -> 153 us
  blocking collectives: 31.3 us -> 0 us
  other arithmetic: 29.3 us -> 6.58 us
  matrix products: 18.1 us -> 0 us
    all_gather x6 -> x0, waiting for transfers between devices: 429 us -> none  [the longest x3 260 us: local(): piece = lax.all_gather(grad_rows, 'dp', axis=0, tiled=True)]
    pallas_call x0 -> x2, Pallas kernels: none -> 153 us  [the longest x1 93.7 us: precondition(): pl.pallas_call(main_kernel, out_shape=(small, small, small, jax.ShapeDtyp...]
    unnamed x9 -> x2, waiting for transfers between devices: 149 us -> 0.7 us
    psum x0 -> x1, waiting for transfers between devices: none -> 76.5 us  [local(): summed = lax.psum(grad_parts[0], 'own')]
    psum x1 -> x0, blocking collectives: 31.3 us -> none  [local(): lax.psum((jnp.stack(adam_sums), jnp.stack(pre_sums)), 'dp')]
    dot_general x9 -> x0, matrix products: 18.1 us -> none  [the longest x3 12.7 us: local(): jnp.dot(mixed_half, lax.all_gather(right_root[0, slot_pos], 'dp', axis=0,...]
    convert_element_type x2 -> x0, other arithmetic: 12.3 us -> none  [the longest x1 11.3 us: local(): packed.astype(jnp.bfloat16)]
  transfers between devices with their start and end apart: 8 -> 2, of which waited for: 7 -> 2; matrix products, arithmetic and copies ran while one was open for 3% -> 1% of each run, Pallas kernels for 0% -> 19%
where the time goes in v1:
time: 309 us
  Pallas kernels  153 us (50%)
  waiting for transfers between devices  127 us (41%)
  between operations  14.2 us (5%)
  local copies, waits for them, and re-layouts  8.28 us (3%)
  other arithmetic  6.58 us (2%)
    pallas_call x1, Pallas kernels, precondition(): pl.pallas_call(main_kernel, out_shape=(small, small, small, jax.ShapeDtyp...  93.7 us
    psum x1, waiting for transfers between devices, local(): summed = lax.psum(grad_parts[0], 'own')  76.5 us
    pallas_call x1, Pallas kernels, gather_roots(): pl.pallas_call(roots_kernel, out_shape=(jax.ShapeDtypeStruct((SLOTS, ROWS...  59.4 us
    all_gather x1, waiting for transfers between devices, local(): every_rows = lax.all_gather(new_rows, 'own', axis=0, tiled=True)  49.8 us
  transfers between devices with their start and end apart: 2, of which 2 were waited for; matrix products, arithmetic and copies ran while one was open for 1% of the time, Pallas kernels for 19%

profile of v1, /device:TPU:1, one launch (start us, length us, event | category | flops | bytes accessed | tf_op | source)
XLA Modules:
  0.0 309.2 jit_solution(5679901749684303937)
XLA Ops:
  7.2 0.0 all-reduce.3.cloned.1.call-start
  7.2 0.7 all-reduce.3.cloned.1.call-update
  7.9 0.0 all-gather.2.cloned.1.call-start
  8.0 0.2 convert_reduce_fusion.1
  8.2 0.1 convert_reduce_fusion
  8.3 0.1 dynamic_slice.6
  8.4 59.4 %gather_roots.1 = (bf16[3,72,1152]{2,1,0:T(8,128)(2,1)}, bf16[3,1152,1152]{2,1,0:T(8,128)(2,1)}) custom-call(bf16[3,72,1152]{2,1,0:T(8,128)(2,1)} %bitcast.19, bf16[3,72,1152]{2,1,0:T(8,128)(2,1)} %bitcast.20), custom_call_target="tpu_custom_call" | custom-call | bytes 100000000 | tf_op jit(solution)/shard_map/gather_roots/pallas_call | solution.py:173
  67.8 0.1 compare_and_fusion.1
  67.9 76.5 %all-reduce.3.cloned.1.call-done = bf16[16,72,1152]{2,1,0:T(8,128)(2,1)} async-done(((bf16[16,72,1152]{2,1,0:T(8,128)(2,1)}), bf16[16,72,1152]{2,1,0:T(8,128)(2,1)}) %all-reduce.3.cloned.1.call-update) | async-done | bytes 2654224 | tf_op jit(solution)/shard_map/psum | solution.py:323
  144.3 2.4 gather_fusion
  146.7 1.5 fusion.5
  148.2 0.1 pad.4
  148.3 0.7 broadcast_in_dim.66.adam_ref
  149.0 93.7 %precondition.1 = (bf16[3,72,1152]{2,1,0:T(8,128)(2,1)}, bf16[3,72,1152]{2,1,0:T(8,128)(2,1)}, bf16[3,72,1152]{2,1,0:T(8,128)(2,1)}, bf16[3,1152,1152]{2,1,0:T(8,128)(2,1)}) custom-call(bf16[3,72,1152]{2,1,0:T(8,128)(2,1)} %get-tuple-element.19.grad_ref, bf16[3,72,1152]{2,1,0:T(8,128)(2,1)} %get-tuple-element.9.left_ref, ...), custom_call_target="tpu_custom_call" | custom-call | tf_op jit(solution)/shard_map/precondition/pallas_call | solution.py:272
  242.7 0.0 copy-start.1
  242.7 0.0 all-gather.2.cloned.1.call-update
  242.8 1.3 fusion.4
  244.0 0.5 copy-done.2
  244.6 0.1 copy-done.3
  244.7 0.2 copy-done.4
  244.8 1.6 bitcast_add_fusion
  246.4 49.8 %all-gather.2.cloned.1.call-done = bf16[48,72,1152]{2,1,0:T(8,128)(2,1)} async-done(((bf16[3,72,1152]{2,1,0:T(8,128)(2,1)}), bf16[48,72,1152]{2,1,0:T(8,128)(2,1)}) %all-gather.2.cloned.1.call-update) | async-done | bytes 7962640 | tf_op jit(solution)/shard_map/all_gather | solution.py:336
  296.3 4.3 %gather_fusion.1 = bf16[16,72,1152]{2,1,0:T(8,128)(2,1)S(1)} fusion(bf16[48,72,1152]{2,1,0:T(8,128)(2,1)} %all-gather.2.cloned.1.call-done, s32[1024]{0:T(1024)S(1)} %pad_clamp_fusion), kind=kCustom, calls=%fused_computation.1 | custom fusion | bytes 5308480 | tf_op jit(solution)/shard_map/jit(_take)/gather | solution.py:337
  300.6 1.8 broadcast_select_fusion
  (13 shorter events, 0.1 us)
Async XLA Ops:
  7.2 0.8 copy-start.5
  7.2 139.5 %copy-start = (f32[1,3,72,1152]{3,2,1,0:T(8,128)S(1)}, f32[1,3,72,1152]{3,2,1,0:T(8,128)}, u32[]{:S(2)}) copy-start(f32[1,3,72,1152]{3,2,1,0:T(8,128)} %param.12) | copy-start | bytes 2985988
  7.2 137.2 %all-reduce.3.cloned.1.call-start = ((), (), s32[]{:S(2)}) async-start(), calls=%async_computation | async-start | bytes 5308416 | tf_op jit(solution)/shard_map/psum | solution.py:323
  7.9 288.4 %all-gather.2.cloned.1.call-start = ((), (), s32[]{:S(2)}) async-start(), calls=%async_computation.1 | async-start | bytes 8460288 | tf_op jit(solution)/shard_map/all_gather | solution.py:336
  242.7 1.3 copy-start.1
  242.7 1.9 copy-start.2
  242.7 2.0 copy-start.3
  242.8 2.1 copy-start.4
Sparse Core Ops, SparseCore 0:
  10.7 133.6 all-reduce.2
  242.9 53.3 all-gather.1

commit v2 on v1

--- a/solution.py
+++ b/solution.py
@@ -27,9 +27,20 @@
         self.fourth = self.at((self.dp + 16 + 2 * (1 - 2 * self.c)) % 16, self.own)
         self.swap = self.at(2 * self.z + self.c, self.own - self.c + self.h)
         self.swaps = self.c != self.h
+        self.x = self.own // 2 % 4
+        self.y = self.own // 8
+        self.x_right = self.at(self.dp, self.chip(0, 1))
+        self.x_left = self.at(self.dp, self.chip(0, -1))
+        self.y_other = self.at(self.dp, self.chip(1, 0))
+        self.way = 1 - 2 * self.c
+        self.x_ahead = self.at(self.dp, self.chip(0, self.way))
+        self.x_behind = self.at(self.dp, self.chip(0, -self.way))
 
     def at(self, dp, own):
         return {"dp": dp, "own": own}
+
+    def chip(self, dy, dx):
+        return 2 * (4 * ((self.y + dy) % 2) + (self.x + dx + 4) % 4) + self.c
 
     def block(self, step, core):
         return 2 * ((self.z + step + ZS) % ZS) + core
@@ -147,154 +158,455 @@
 ]
 
 
-def roots_kernel(left_ref, right_ref, left_out, full_out, swap_send, swap_recv, *sems):
+class OwnGather:
+    PLACES = [(dy, dx) for dy in (0, 1) for dx in (0, 1, -1, 2)]
+
+    def __init__(self, place, window, sems, y_first):
+        self.place, self.window, self.y_first = place, window, y_first
+        self.send_sem, self.recv_sem, self.pair_send, self.pair_recv = sems
+        self.started = []
+
+    def index(self, dy, dx):
+        return self.PLACES.index((dy, dx))
+
+    def put(self, own, dy, dx, device, source=None):
+        i = self.index(dy, dx)
+        window = self.window(own)
+        copy = remote(window if source is None else source, window, self.send_sem.at[i], self.recv_sem.at[i], device)
+        copy.start()
+        self.started.append(copy)
+
+    def hand(self, dy, dx, source=None):
+        i = self.index(dy, dx)
+        window = self.window(self.place.chip(dy, dx))
+        copy = remote(
+            window if source is None else source, window, self.pair_send.at[i], self.pair_recv.at[i], self.place.pair
+        )
+        copy.start()
+        self.started.append(copy)
+
+    def arrive(self, dy, dx):
+        i = self.index(dy, dx)
+        window = self.window(self.place.chip(dy, dx))
+        remote(window, window, self.send_sem.at[i], self.recv_sem.at[i], self.place.pair).wait_recv()
+
+    def begin(self, source):
+        p = self.place
+        own = p.own
+        if self.y_first:
+            self.put(own, 1, 0, p.y_other, source)
+        self.put(own, 0, -1, p.x_right, source)
+        self.put(own, 0, 1, p.x_left, source)
+        if not self.y_first:
+            self.put(own, 1, 0, p.y_other, source)
+        self.hand(0, 0, source)
+
+    def across(self):
+        p = self.place
+        self.arrive(1, 0)
+        if self.y_first:
+            self.put(p.chip(1, 0), 1, -1, p.x_right)
+            self.put(p.chip(1, 0), 1, 1, p.x_left)
+        self.hand(1, 0)
+
+    def near(self, dy):
+        p = self.place
+        self.arrive(dy, -1)
+        self.arrive(dy, 1)
+        if self.y_first or dy == 0:
+            self.put(p.chip(dy, -p.way), dy, 2, p.x_ahead)
+        if dy == 0 and not self.y_first:
+            self.put(p.chip(0, -1), 1, -1, p.y_other)
+            self.put(p.chip(0, 1), 1, 1, p.y_other)
+        self.hand(dy, -1)
+        self.hand(dy, 1)
+
+    def far(self, dy):
+        self.arrive(dy, 2)
+        if dy == 0 and not self.y_first:
+            self.put(self.place.chip(0, 2), 1, 2, self.place.y_other)
+        self.hand(dy, 2)
+
+    def handed(self):
+        p = self.place
+        for dy, dx in self.PLACES:
+            i = self.index(dy, dx)
+            window = self.window(p.chip(dy, dx) + 1 - 2 * p.c)
+            remote(window, window, self.pair_send.at[i], self.pair_recv.at[i], p.pair).wait_recv()
+
+    def finish(self):
+        for copy in self.started:
+            copy.wait_send()
+
+
+OWN_SEMS = [pltpu.SemaphoreType.DMA((8,))] * 4
+
+
+class OwnSum:
+    def __init__(self, place, parts, buffers, sems):
+        self.place, self.parts = place, parts
+        self.mine, self.inbox, self.chip_sum, self.relay, self.mail, self.total = buffers
+        self.load_sem, self.core_send, self.core_recv, self.mail_send, self.mail_recv = sems
+        self.started = []
+
+    def unit(self, ky, dx):
+        return 4 * ky + (self.place.x + dx + 4) % 4
+
+    def begin(self):
+        p = self.place
+        for dx in (2, p.way, -p.way, 0):
+            for ky in range(2):
+                k = self.unit(ky, dx)
+                copy = remote(self.parts.at[k, 1 - p.c], self.inbox.at[k], self.core_send.at[k], self.core_recv.at[k], p.pair)
+                copy.start()
+                self.started.append(copy)
+        for dx in (2, -p.way, p.way, 0):
+            for ky in range(2):
+                k = self.unit(ky, dx)
+                pltpu.make_async_copy(self.parts.at[k, p.c], self.mine.at[k], self.load_sem.at[k]).start()
+
+    def of_chip(self, ky, dx):
+        p = self.place
+        k = self.unit(ky, dx)
+        remote(self.parts.at[k, p.c], self.inbox.at[k], self.core_send.at[k], self.core_recv.at[k], p.pair).wait_recv()
+        pltpu.make_async_copy(self.parts.at[k, p.c], self.mine.at[k], self.load_sem.at[k]).wait()
+        return self.mine[k].astype(jnp.float32) + self.inbox[k].astype(jnp.float32)
+
+    def post(self, source, index, device):
+        copy = remote(source, self.mail.at[index], self.mail_send.at[index], self.mail_recv.at[index], device)
+        copy.start()
+        self.started.append(copy)
+
+    def receive(self, index):
+        window = self.mail.at[index]
+        remote(window, window, self.mail_send.at[index], self.mail_recv.at[index], self.place.pair).wait_recv()
+        return self.mail[index].astype(jnp.float32)
+
+    def out_far(self, ky):
+        self.chip_sum[ky] = self.of_chip(ky, 2).astype(jnp.bfloat16)
+        self.post(self.chip_sum.at[ky], ky, self.place.x_ahead)
+
+    def out_near(self, ky):
+        self.chip_sum[2 + ky] = self.of_chip(ky, -self.place.way).astype(jnp.bfloat16)
+        self.post(self.chip_sum.at[2 + ky], 2 + ky, self.place.x_behind)
+
+    def on(self, ky):
+        own = self.of_chip(ky, self.place.way)
+        self.relay[ky] = (self.receive(ky) + own).astype(jnp.bfloat16)
+        self.post(self.relay.at[ky], 4 + ky, self.place.x_ahead)
+
+    def cross(self):
+        p = self.place
+        ky = 1 - p.y
+        own = self.of_chip(ky, 0)
+        self.relay[2] = (own + self.receive(2 + ky) + self.receive(4 + ky)).astype(jnp.bfloat16)
+        self.post(self.relay.at[2], 6, p.y_other)
+
+    def end(self):
+        p = self.place
+        own = self.of_chip(p.y, 0) + self.receive(2 + p.y) + self.receive(4 + p.y)
+        self.total[...] = (own + self.receive(6)).astype(jnp.bfloat16)
+
+    def finish(self):
+        for copy in self.started:
+            copy.wait_send()
+
+
+def block_buffer(count):
+    return pltpu.VMEM((count, ROWS, WIDTH), jnp.bfloat16)
+
+
+SUM_SCRATCH = [
+    block_buffer(8),
+    block_buffer(8),
+    block_buffer(4),
+    block_buffer(3),
+    block_buffer(7),
+    pltpu.VMEM((ROWS, WIDTH), jnp.bfloat16),
+    pltpu.SemaphoreType.DMA((8,)),
+    pltpu.SemaphoreType.DMA((8,)),
+    pltpu.SemaphoreType.DMA((8,)),
+    pltpu.SemaphoreType.DMA((7,)),
+    pltpu.SemaphoreType.DMA((7,)),
+]
+
+
+def roots_kernel(parts_ref, left_ref, right_ref, left_out, full_out, sum_out, swap_send, swap_recv, own_sem, *rest):
+    ring_sems, gather_sems, sum_scratch = rest[:4], rest[4:8], rest[8:]
     place = Place()
-    greet(place, [place.right, place.left, place.pair])
+    greet(place, [place.right, place.left, place.pair, place.x_right, place.x_left, place.y_other])
+    total = OwnSum(place, parts_ref, sum_scratch[:6], sum_scratch[6:])
+    total.begin()
     moves = [(right_ref.at[s], full_out.at[s, rows(place.dp)]) for s in range(SLOTS)]
     moves += [(left_ref.at[s], left_out.at[s]) for s in range(SLOTS)]
     exchange(place, moves, swap_send, swap_recv)
-    ring = Ring(place, full_out, sems)
-    for slot in range(SLOTS):
+    ring = Ring(place, full_out, ring_sems)
+
+    def begin(slot):
         src, _ = moves[slot]
         exchange_wait(place, slot, src, full_out.at[slot, rows(place.block(0, place.c))], swap_send, swap_recv)
         ring.begin(slot)
-    for k in range(1, 5):
-        for slot in range(SLOTS):
-            ring.hop(k, slot)
+
+    every = OwnGather(place, lambda own: sum_out.at[own], gather_sems, True)
+    total.out_far(0)
+    total.out_far(1)
+    begin(0)
+    total.out_near(0)
+    total.out_near(1)
+    begin(1)
+    total.on(0)
+    begin(2)
+    ring.hop(1, 0)
+    total.on(1)
+    ring.hop(1, 1)
+    total.cross()
+    ring.hop(1, 2)
+    total.end()
+    every.begin(total.total)
+    keep = pltpu.make_async_copy(total.total, sum_out.at[place.own], own_sem)
+    keep.start()
+    ring.hop(2, 0)
+    every.across()
+    ring.hop(2, 1)
+    every.near(0)
+    ring.hop(2, 2)
+    every.near(1)
+    ring.hop(3, 0)
+    every.far(0)
+    ring.hop(3, 1)
+    every.far(1)
+    ring.hop(3, 2)
+    for slot in range(SLOTS):
+        ring.hop(4, slot)
+    every.handed()
     for slot in range(SLOTS):
         ring.handed(slot)
         src, dst = moves[SLOTS + slot]
         exchange_wait(place, SLOTS + slot, src, dst, swap_send, swap_recv)
-    ring.finish()
-
-
-def gather_roots(left_root, right_root):
+    keep.wait()
+    for part in (total, every, ring):
+        part.finish()
+
+
+def gather_roots(parts, left_root, right_root):
     anywhere = pl.BlockSpec(memory_space=pl.ANY)
     return pl.pallas_call(
         roots_kernel,
         out_shape=(
             jax.ShapeDtypeStruct((SLOTS, ROWS, WIDTH), jnp.bfloat16),
             jax.ShapeDtypeStruct((SLOTS, WIDTH, WIDTH), jnp.bfloat16),
+            jax.ShapeDtypeStruct((16, ROWS, WIDTH), jnp.bfloat16),
         ),
-        in_specs=[anywhere, anywhere],
-        out_specs=(anywhere, anywhere),
+        in_specs=[anywhere] * 3,
+        out_specs=(anywhere,) * 3,
         scratch_shapes=[
             pltpu.SemaphoreType.DMA((2 * SLOTS,)),
             pltpu.SemaphoreType.DMA((2 * SLOTS,)),
+            pltpu.SemaphoreType.DMA,
             *RING_SEMS,
+            *OWN_SEMS,
+            *SUM_SCRATCH,
         ],
         compiler_params=pltpu.CompilerParams(collective_id=0, has_side_effects=True),
-        cost_estimate=pl.CostEstimate(flops=0, bytes_accessed=100_000_000, transcendentals=0),
         name="gather_roots",
-    )(left_root, right_root)
+    )(parts, left_root, right_root)
 
 
 NT = (((1,), (1,)), ((), ()))
 
 
 def main_kernel(
-    grad_ref, left_ref, right_ref, weight_ref, adam_ref,
+    slot_ref, grad_ref, left_ref, right_ref, weight_ref, adam_ref,
     gram_left_ref, gram_right_ref, new_ref, full_hbm,
-    full, right_full, results, returned, sums, totals,
+    full, right_full, results, returned, updated, every, sums, totals,
     swap_send, swap_recv, back_send, back_recv, local_sem, sum_send, sum_recv, *sems
 ):
     place = Place()
     peers = [place.at((place.dp + d) % 16, place.own) for d in range(1, 16)]
-    greet(place, [place.pair, *peers])
+    greet(place, [place.pair, place.x_right, place.x_left, place.y_other, *peers])
+    moves = [(grad_ref.at[s], full_hbm.at[s, rows(place.dp)]) for s in range(SLOTS)]
+    exchange(place, moves, swap_send, swap_recv)
     load_right = pltpu.make_async_copy(right_ref, right_full, local_sem.at[0])
     load_right.start()
-    moves = [(grad_ref.at[s], full_hbm.at[s, rows(place.dp)]) for s in range(SLOTS)]
-    exchange(place, moves, swap_send, swap_recv)
-    ring = Ring(place, full_hbm, sems)
+    ring = Ring(place, full_hbm, sems[:4])
     work = place.block(0, place.c)
-    for slot in range(SLOTS):
+    lane = lax.broadcasted_iota(jnp.int32, (ROWS, WIDTH), 1)
+    row = lax.broadcasted_iota(jnp.int32, (ROWS, WIDTH), 0)
+    pick = jnp.where(lane == row + work * ROWS, 1.0, 0.0).astype(jnp.bfloat16)
+
+    def begin(slot):
         src, _ = moves[slot]
         exchange_wait(place, slot, src, full_hbm.at[slot, rows(work)], swap_send, swap_recv)
         ring.begin(slot)
-    for k in range(1, 5):
-        for slot in range(SLOTS):
-            ring.hop(k, slot)
-    for slot in range(SLOTS):
-        ring.handed(slot)
-        pltpu.make_async_copy(full_hbm.at[slot], full.at[slot], local_sem.at[1 + slot]).start()
-    ring.finish()
-    load_right.wait()
-    lane = lax.broadcasted_iota(jnp.int32, (ROWS, WIDTH), 1)
-    row = lax.broadcasted_iota(jnp.int32, (ROWS, WIDTH), 0)
-    pick = jnp.where(lane == row + work * ROWS, 1.0, 0.0).astype(jnp.bfloat16)
-    for slot in range(SLOTS):
-        pltpu.make_async_copy(full_hbm.at[slot], full.at[slot], local_sem.at[1 + slot]).wait()
-
-    def compute(slot, carry):
+
+    def load(slot):
+        return pltpu.make_async_copy(full_hbm.at[slot], full.at[slot], local_sem.at[1 + slot])
+
+    back = {}
+    for s in range(SLOTS):
+        back[s, 0] = (results.at[s, 0], gram_left_ref.at[s])
+        back[s, 1] = (results.at[s, 1], gram_right_ref.at[s])
+        back[s, 2] = (results.at[s, 2], returned.at[s])
+
+    def give(slot, which):
+        i = 3 * slot + which
+        exchange(place, [back[slot, which]], back_send.at[pl.ds(i, 1)], back_recv.at[pl.ds(i, 1)])
+
+    def given(slot, which):
+        exchange_wait(place, 3 * slot + which, *back[slot, which], back_send, back_recv)
+
+    def solve(slot):
+        mixed = jnp.dot(left_ref[slot], full[slot], preferred_element_type=jnp.float32).astype(jnp.bfloat16)
+        precond = jnp.dot(mixed, right_full[slot], preferred_element_type=jnp.float32)
+        results[slot, 2] = precond.astype(jnp.bfloat16)
+
+    def grams(slot):
         grad = full[slot]
         mine = jnp.dot(pick, grad, preferred_element_type=jnp.float32).astype(jnp.bfloat16)
         results[slot, 0] = lax.dot_general(mine, grad, NT, preferred_element_type=jnp.float32).astype(jnp.bfloat16)
         columns = lax.dot_general(pick, grad, NT, preferred_element_type=jnp.float32).astype(jnp.bfloat16)
         results[slot, 1] = jnp.dot(columns, grad, preferred_element_type=jnp.float32).astype(jnp.bfloat16)
-        mixed = jnp.dot(left_ref[slot], grad, preferred_element_type=jnp.float32).astype(jnp.bfloat16)
-        precond = jnp.dot(mixed, right_full[slot], preferred_element_type=jnp.float32)
-        results[slot, 2] = precond.astype(jnp.bfloat16)
-        return carry
-
-    lax.fori_loop(0, SLOTS, compute, 0)
-    back = [(results.at[s, i], returned.at[s, i]) for s in range(SLOTS) for i in (2, 0, 1)]
-    exchange(place, back, back_send, back_recv)
-    for i, (src, dst) in enumerate(back):
-        exchange_wait(place, i, src, dst, back_send, back_recv)
-
-    spread = jnp.zeros((8, 128), jnp.float32)
+
+    begin(0)
+    begin(1)
+    ring.hop(1, 0)
+    begin(2)
+    ring.hop(1, 1)
+    ring.hop(2, 0)
+    ring.hop(1, 2)
+    ring.hop(2, 1)
+    ring.hop(3, 0)
+    ring.hop(2, 2)
+    ring.hop(3, 1)
+    ring.hop(4, 0)
+    ring.handed(0)
+    load(0).start()
+    load_right.wait()
+    load(0).wait()
+    solve(0)
+    give(0, 2)
+    ring.hop(3, 2)
+    ring.hop(4, 1)
+    grams(0)
+    give(0, 0)
+    give(0, 1)
+    ring.hop(4, 2)
+    ring.handed(1)
+    load(1).start()
+    ring.handed(2)
+    load(2).start()
+    load(1).wait()
+    solve(1)
+    give(1, 2)
+    load(2).wait()
+    solve(2)
+    give(2, 2)
+    grams(1)
+    give(1, 0)
+    give(1, 1)
+
+    spread = adam_ref[...]
     index = lax.broadcasted_iota(jnp.int32, (8, 128), 0)
     for slot in range(SLOTS):
-        precond = returned[slot, 2].astype(jnp.float32)
+        given(slot, 2)
+        precond = returned[slot].astype(jnp.float32)
         spread = spread + jnp.where(index == slot, jnp.sum(precond * precond), 0.0)
-    sums[...] = spread + adam_ref[...]
+    sums[...] = spread
     copies = []
     for d, peer in enumerate(peers):
         copies.append(remote(sums, totals.at[d], sum_send.at[d], sum_recv.at[d], peer))
         copies[-1].start()
-    gram_left_ref[...] = returned[:, 0]
-    gram_right_ref[...] = returned[:, 1]
+    grams(2)
+    give(2, 0)
+    give(2, 1)
     total = sums[...]
     for d, copy in enumerate(copies):
-        copy.wait()
+        copy.wait_recv()
         total = total + totals[d]
+
+    gathers = []
+    for slot in range(SLOTS):
+        window = functools.partial(lambda slot, own: every.at[SLOTS * own + slot], slot)
+        own_sems = [sem.at[slot] for sem in sems[4:8]]
+        gathers.append(OwnGather(place, window, own_sems, slot > 0))
     for slot in range(SLOTS):
         pre_total, adam_total = total[slot : slot + 1, 0:1], total[slot + 3 : slot + 4, 0:1]
         graft = jnp.sqrt(adam_total / (pre_total + 1e-06))
-        precond = returned[slot, 2].astype(jnp.float32)
-        new_ref[slot] = (weight_ref[slot].astype(jnp.float32) - 0.3 * graft * precond).astype(jnp.bfloat16)
-
-
-def precondition(grads, left_rows, right_full, weights, adam):
+        precond = returned[slot].astype(jnp.float32)
+        updated[slot] = (weight_ref[slot].astype(jnp.float32) - 0.3 * graft * precond).astype(jnp.bfloat16)
+        gathers[slot].begin(updated.at[slot])
+        pltpu.make_async_copy(updated.at[slot], every.at[SLOTS * place.own + slot], local_sem.at[4 + slot]).start()
+    gathers[0].near(0)
+    gathers[1].across()
+    gathers[2].across()
+    gathers[1].near(0)
+    gathers[2].near(0)
+    gathers[0].across()
+    gathers[0].far(0)
+    gathers[1].near(1)
+    gathers[2].near(1)
+    gathers[0].near(1)
+    gathers[1].far(0)
+    gathers[2].far(0)
+    gathers[0].far(1)
+    gathers[1].far(1)
+    gathers[2].far(1)
+    for slot in range(SLOTS):
+        gathers[slot].handed()
+        pltpu.make_async_copy(updated.at[slot], every.at[SLOTS * place.own + slot], local_sem.at[4 + slot]).wait()
+
+    def place_unit(unit, carry):
+        new_ref[unit] = every[slot_ref[unit]]
+        return carry
+
+    lax.fori_loop(0, 16, place_unit, 0)
+    for slot in range(SLOTS):
+        given(slot, 0)
+        given(slot, 1)
+        gathers[slot].finish()
+    ring.finish()
+    for copy in copies:
+        copy.wait_send()
+
+
+def precondition(slot_id, grads, left_rows, right_full, weights, adam):
     anywhere = pl.BlockSpec(memory_space=pl.ANY)
     vmem = pl.BlockSpec(memory_space=pltpu.VMEM)
     small = jax.ShapeDtypeStruct((SLOTS, ROWS, WIDTH), jnp.bfloat16)
     return pl.pallas_call(
         main_kernel,
-        out_shape=(small, small, small, jax.ShapeDtypeStruct((SLOTS, WIDTH, WIDTH), jnp.bfloat16)),
-        in_specs=[anywhere, vmem, anywhere, vmem, vmem],
+        out_shape=(
+            small,
+            small,
+            jax.ShapeDtypeStruct((16, ROWS, WIDTH), jnp.bfloat16),
+            jax.ShapeDtypeStruct((SLOTS, WIDTH, WIDTH), jnp.bfloat16),
+        ),
+        in_specs=[pl.BlockSpec(memory_space=pltpu.SMEM), anywhere, vmem, anywhere, vmem, vmem],
         out_specs=(vmem, vmem, vmem, anywhere),
         scratch_shapes=[
             pltpu.VMEM((SLOTS, WIDTH, WIDTH), jnp.bfloat16),
             pltpu.VMEM((SLOTS, WIDTH, WIDTH), jnp.bfloat16),
             pltpu.VMEM((SLOTS, 3, ROWS, WIDTH), jnp.bfloat16),
-            pltpu.VMEM((SLOTS, 3, ROWS, WIDTH), jnp.bfloat16),
+            block_buffer(SLOTS),
+            block_buffer(SLOTS),
+            block_buffer(16 * SLOTS),
             pltpu.VMEM((8, 128), jnp.float32),
             pltpu.VMEM((15, 8, 128), jnp.float32),
             pltpu.SemaphoreType.DMA((SLOTS,)),
             pltpu.SemaphoreType.DMA((SLOTS,)),
             pltpu.SemaphoreType.DMA((3 * SLOTS,)),
             pltpu.SemaphoreType.DMA((3 * SLOTS,)),
-            pltpu.SemaphoreType.DMA((1 + SLOTS,)),
+            pltpu.SemaphoreType.DMA((1 + 2 * SLOTS,)),
             pltpu.SemaphoreType.DMA((15,)),
             pltpu.SemaphoreType.DMA((15,)),
             *RING_SEMS,
+            *[pltpu.SemaphoreType.DMA((SLOTS, 8))] * 4,
         ],
         compiler_params=pltpu.CompilerParams(
             collective_id=1, has_side_effects=True, vmem_limit_bytes=60 * 1024 * 1024
         ),
         name="precondition",
-    )(grads, left_rows, right_full, weights, adam)
+    )(slot_id, grads, left_rows, right_full, weights, adam)
 
 
 def slot_tables(owner_list, owner_count, slot_count, unit_count):
@@ -319,8 +631,8 @@
     units = lax.dynamic_slice_in_dim(unit_of_slot, me * SLOTS, SLOTS)
     mine = lax.dynamic_slice_in_dim(filled, me * SLOTS, SLOTS)
 
-    left_rows, right_full = gather_roots(left_root[0], right_root[0])
-    summed = lax.psum(grad_parts[0], "own")
+    parts = grad_parts.reshape(8, 2, ROWS, WIDTH)
+    left_rows, right_full, summed = gather_roots(parts, left_root[0], right_root[0])
     grads = jnp.where(mine[:, None, None], jnp.take(summed, units, axis=0), jnp.bfloat16(0.0))
 
     gradient = grads.astype(jnp.float32)
@@ -329,12 +641,10 @@
     adam_sums = jnp.sum(adam * adam, axis=(1, 2))
     adam_tile = jnp.broadcast_to(jnp.pad(adam_sums, (3, 2))[:, None], (8, 128))
 
-    gram_left, gram_right, new_rows, _ = precondition(grads, left_rows, right_full, weights[0], adam_tile)
+    gram_left, gram_right, new_weights, _ = precondition(slot_id, grads, left_rows, right_full, weights[0], adam_tile)
     scale = 0.05 / WIDTH
     new_left = 0.95 * left_stat + scale * gram_left.astype(jnp.float32)[None]
     new_right = 0.95 * right_stat + scale * gram_right.astype(jnp.float32)[None]
-    every_rows = lax.all_gather(new_rows, "own", axis=0, tiled=True)
-    new_weights = jnp.take(every_rows, slot_id, axis=0)
     return (new_left, new_right, new_second[None], new_weights)
 
 

time: 309 us -> 178 us (0.58)
  waiting for transfers between devices: 127 us -> 0 us
  between operations: 14.2 us -> 0.7 us
  Pallas kernels: 153 us -> 164 us
  local copies, waits for them, and re-layouts: 8.28 us -> 4.72 us
    psum x1 -> x0, waiting for transfers between devices: 76.5 us -> none  [local(): summed = lax.psum(grad_parts[0], 'own')]
    all_gather x1 -> x0, waiting for transfers between devices: 49.8 us -> none  [local(): every_rows = lax.all_gather(new_rows, 'own', axis=0, tiled=True)]
    pallas_call x1, Pallas kernels: 93.7 us -> 104 us  [precondition(): pl.pallas_call(main_kernel, out_shape=(small, small, jax.ShapeDtypeStruct...]
    gather x1 -> x0, local copies, waits for them, and re-layouts: 4.26 us -> none  [local(): new_weights = jnp.take(every_rows, slot_id, axis=0)]
  transfers between devices with their start and end apart: 2 -> 0, of which waited for: 2 -> 0; matrix products, arithmetic and copies ran while one was open for 1% -> 0% of each run, Pallas kernels for 19% -> 0%
where the time goes in v2:
time: 178 us; the launch traced here: 177 us
  Pallas kernels  164 us (92%)
  other arithmetic  7.46 us (4%)
  local copies, waits for them, and re-layouts  4.72 us (3%)
    pallas_call x1, Pallas kernels, precondition(): pl.pallas_call(main_kernel, out_shape=(small, small, jax.ShapeDtypeStruct...  104 us
    pallas_call x1, Pallas kernels, gather_roots(): pl.pallas_call(roots_kernel, out_shape=(jax.ShapeDtypeStruct((SLOTS, ROWS...  60.2 us

profile of v2, /device:TPU:1, one launch (start us, length us, event | category | flops | bytes accessed | tf_op | source)
XLA Modules:
  0.0 177.2 jit_solution(10490573476101411748)
XLA Ops:
  0.6 0.0 copy-start
  0.6 0.9 convert_reduce_fusion.1
  1.6 0.7 multiply_add_fusion.slot_ref
  2.2 0.0 copy-start.4
  2.2 0.1 convert_reduce_fusion
  2.3 0.1 compare_and_fusion
  2.4 60.2 %gather_roots.1 = (bf16[3,72,1152]{2,1,0:T(8,128)(2,1)}, bf16[3,1152,1152]{2,1,0:T(8,128)(2,1)}, bf16[16,72,1152]{2,1,0:T(8,128)(2,1)}) custom-call(bf16[8,2,72,1152]{3,2,1,0:T(8,128)(2,1)} %bitcast.18, bf16[3,72,1152]{2,1,0:T(8,128)(2,1)} %bitcast.19, bf16[3,72,1152]{2,1,0:T(8,128)(2,1)} %bitcast.20), custom_call_target="tpu_custom_call" | custom-call | tf_op jit(solution)/shard_map/gather_roots/pallas_call | solution.py:393
  62.6 2.4 %gather_fusion = bf16[3,72,1152]{2,1,0:T(8,128)(2,1)S(1)} fusion(bf16[16,72,1152]{2,1,0:T(8,128)(2,1)} %get-tuple-element.10, s32[1024]{0:T(1024)S(1)} %pad_clamp_fusion), kind=kCustom, calls=%fused_computation | custom fusion | bytes 995340 | tf_op jit(solution)/shard_map/jit(_take)/gather | solution.py:636
  65.0 0.1 dynamic_slice.6
  65.1 0.0 copy-done
  65.1 1.5 fusion.5
  66.6 0.0 copy-done.4
  66.6 0.1 pad.4
  66.7 0.7 broadcast_in_dim.54.adam_ref
  67.3 0.0 copy-start.2
  67.3 0.0 copy-start.3
  67.4 104.2 %precondition.1 = (bf16[3,72,1152]{2,1,0:T(8,128)(2,1)}, bf16[3,72,1152]{2,1,0:T(8,128)(2,1)}, bf16[16,72,1152]{2,1,0:T(8,128)(2,1)}, bf16[3,1152,1152]{2,1,0:T(8,128)(2,1)}) custom-call(s32[16]{0:T(128)} %copy-done.4, bf16[3,72,1152]{2,1,0:T(8,128)(2,1)} %get-tuple-element.19.grad_ref, bf16[3,72,1152]{2,1,0:T(8,128)(2,1)} %get-tuple-element.11.left_ref, ...), custom_call_target="tpu_custom_call" | custom-call | tf_op jit(solution)/shard_map/precondition/pallas_call | solution.py:576
  171.5 0.0 copy-done.2
  171.5 0.0 copy-done.3
  171.5 0.0 copy-start.1
  171.6 2.9 %bitcast_add_fusion = (f32[1,3,72,1152]{3,2,1,0:T(8,128)}, f32[1,3,72,1152]{3,2,1,0:T(8,128)}) fusion(bf16[3,72,1152]{2,1,0:T(8,128)(2,1)} %get-tuple-element.14, f32[1,3,72,1152]{3,2,1,0:T(8,128)S(1)} %copy-done.2, bf16[3,72,1152]{2,1,0:T(8,128)(2,1)} %get-tuple-element.13, f32[1,3,72,1152]{3,2,1,0:T(8,128)S(1)} %copy-done.3), kind=kLoop, calls=%fused_computation.9 | loop fusion | flops 1990656 | bytes 4976640 | tf_op jit(solution)/shard_map/add | solution.py:647
  174.5 1.2 fusion.4
  175.7 0.0 copy-done.1
  175.7 1.5 copy.13
  (2 shorter events, 0.0 us)
Async XLA Ops:
  0.6 64.5 %copy-start = (f32[1,3,72,1152]{3,2,1,0:T(8,128)S(1)}, f32[1,3,72,1152]{3,2,1,0:T(8,128)}, u32[]{:S(2)}) copy-start(f32[1,3,72,1152]{3,2,1,0:T(8,128)} %param.12) | copy-start | bytes 2985988
  2.2 64.4 %copy-start.4 = (s32[16]{0:T(128)}, s32[16]{0:T(128)S(1)}, u32[]{:S(2)}) copy-start(s32[16]{0:T(128)S(1)} %multiply_add_fusion.slot_ref) | copy-start | bytes 196
  67.3 104.2 %copy-start.2 = (f32[1,3,72,1152]{3,2,1,0:T(8,128)S(1)}, f32[1,3,72,1152]{3,2,1,0:T(8,128)}, u32[]{:S(2)}) copy-start(f32[1,3,72,1152]{3,2,1,0:T(8,128)} %param.11) | copy-start | bytes 2985988
  67.3 104.2 %copy-start.3 = (f32[1,3,72,1152]{3,2,1,0:T(8,128)S(1)}, f32[1,3,72,1152]{3,2,1,0:T(8,128)}, u32[]{:S(2)}) copy-start(f32[1,3,72,1152]{3,2,1,0:T(8,128)} %param.10) | copy-start | bytes 2985988
  171.5 4.2 %copy-start.1 = (bf16[16,72,1152]{2,1,0:T(8,128)(2,1)S(1)}, bf16[16,72,1152]{2,1,0:T(8,128)(2,1)}, u32[]{:S(2)}) copy-start(bf16[16,72,1152]{2,1,0:T(8,128)(2,1)} %get-tuple-element.31) | copy-start | bytes 7962628
